TPU v7x, 256 devices: a whole 4x4x8 slice. The times are simulated.
256 devices in a mesh: ctx: 32 (over y, x, core), head: 8 (over z).
Axes of the slice: x: 4, y: 4, z: 8, core: 2. Of those that a mesh axis runs over, the one named last changes fastest.
Arguments:
- hidden_in: bfloat16 [8192, 2048], P('ctx'), may hold values from -6 to 6
- gain_attn: float32 [2048], replicated, may hold values from 0.1 to 1.9
- w_qkv: bfloat16 [2048, 3, 2048], P(None, None, 'head'), may hold values from -0.125 to 0.125
- conv_w: float32 [4, 3, 2048], P(None, None, 'head'), may hold values from -3 to 3
- log_decay: float32 [8192, 16], P('ctx', 'head'), may hold values from -1 to 0, as said below
- norm_gain: float32 [2048], P('head'), may hold values from 0.1 to 1.9
- w_out: bfloat16 [2048, 2048], P('head'), may hold values from -0.125 to 0.125
- gain_moe: float32 [2048], replicated, may hold values from 0.1 to 1.9
- expert_ids: int32 [8192, 8], P('ctx'), may hold values from 0 to 63, all different within a row; in each aligned block of 256 rows (0 to 255, 256 to 511, ...) at most 48 rows name the same one
- route_weights: float32 [8192, 8], P('ctx'), may hold values from 0.05 to 1
- w_gate: bfloat16 [256, 2048, 256], P(('ctx', 'head')), may hold values from -0.125 to 0.125
- w_up: bfloat16 [256, 2048, 256], P(('ctx', 'head')), may hold values from -0.125 to 0.125
- w_down: bfloat16 [256, 256, 2048], P(('ctx', 'head')), may hold values from -0.1875 to 0.1875
- grad_core: bfloat16 [8192, 2048], P('ctx', 'head'), may hold values from -6 to 6
Outputs:
- layer_out: bfloat16 [8192, 2048], P('ctx', 'head')
- grad_q: bfloat16 [8192, 2048], P('ctx', 'head')
- grad_k: bfloat16 [8192, 2048], P('ctx', 'head')
- grad_v: bfloat16 [8192, 2048], P('ctx', 'head')
Inputs may be any that keep to these rules, and one draw needn't show every extreme that they name: `expert_ids`: in each aligned block of 256 rows (the tokens of one index of ctx) no expert is chosen by more than 48 rows, a bound that some block reaches; the 8 experts of a row differ. `log_decay`: every entry is negative.
All inputs are finite; a program needn't handle non-finite values.
Results may differ from a plain program's by a relative error of at most 0.023.
Values may be sent and summed in bfloat16 or wider, within the bound.
A program may use at most 128 MiB of HBM per device.

v0:
```python
import jax
import jax.numpy as jnp
from jax import lax
from jax.sharding import PartitionSpec as P

KERNEL = 4
TOP = 8
EXP_CTX = 2


def shifted(value, axis, steps):
    count = lax.axis_size(axis)
    first, last = (max(0, -steps), min(count, count - steps))
    return lax.ppermute(value, axis, [(source, source + steps) for source in range(first, last)])


def entering(value, axis, join, neutral, backward):
    count, mine = (lax.axis_size(axis), lax.axis_index(axis))
    pieces = jax.tree.map(lambda part: lax.all_gather(part, axis), value)
    if backward:
        pieces = jax.tree.map(lambda part: part[::-1], pieces)
        mine = count - 1 - mine
    total = jax.tree.map(
        lambda part, zero: jnp.full_like(part, 0) + jnp.asarray(zero, part.dtype), value, neutral
    )

    def hop(position, total):
        longer = join(total, jax.tree.map(lambda part: part[position], pieces))
        return jax.tree.map(lambda new, old: jnp.where(position < mine, new, old), longer, total)

    return lax.fori_loop(0, count - 1, hop, total)


def rms_norm(values, gain):
    return values * lax.rsqrt(jnp.mean(values * values, axis=-1, keepdims=True) + 1e-06) * gain


def link(earlier, later):
    return (earlier[0] * later[0], later[0][:, None, None] * earlier[1] + later[1])


def body(
    hidden_in,
    gain_attn,
    w_qkv,
    conv_w,
    log_decay,
    norm_gain,
    w_out,
    gain_moe,
    expert_ids,
    route_weights,
    w_gate,
    w_up,
    w_down,
    grad_core,
):
    hi = lax.Precision.HIGHEST
    n_ctx = lax.axis_size("ctx")
    n_head = lax.axis_size("head")
    my_head = lax.axis_index("head")
    tok_dev, width = hidden_in.shape
    chans = w_qkv.shape[2]
    heads_here = log_decay.shape[1]
    head_size = chans // heads_here
    experts = EXP_CTX * n_ctx
    cap = 3 * tok_dev * TOP // (2 * experts)
    shards = n_head // EXP_CTX
    local_expert = my_head // shards
    cols = width // n_head
    x_float = hidden_in.astype(jnp.float32)
    normed = rms_norm(x_float, gain_attn).astype(jnp.bfloat16)
    mixed = jnp.einsum("ti,icj->tcj", normed, w_qkv, preferred_element_type=jnp.float32).astype(
        jnp.bfloat16
    )
    rim = shifted(mixed[tok_dev - (KERNEL - 1) :], "ctx", 1)
    padded = jnp.concatenate([rim, mixed], axis=0).astype(jnp.float32)
    conv_out = jnp.zeros(mixed.shape, jnp.float32)
    for offset in range(KERNEL):
        conv_out = (
            conv_out + conv_w[offset] * padded[KERNEL - 1 - offset : KERNEL - 1 - offset + tok_dev]
        )
    activ = jax.nn.silu(conv_out)
    shape3 = (tok_dev, heads_here, head_size)
    queries = (activ[:, 0] * head_size ** (-0.5)).astype(jnp.bfloat16).reshape(shape3)
    key_rows = activ[:, 1].astype(jnp.bfloat16).reshape(shape3)
    val_rows = activ[:, 2].astype(jnp.bfloat16).reshape(shape3)
    query_f = queries.astype(jnp.float32)
    key_f = key_rows.astype(jnp.float32)
    value_f = val_rows.astype(jnp.float32)
    cot_rows = grad_core.reshape(shape3)
    cot_f = cot_rows.astype(jnp.float32)
    cum_decay = jnp.cumsum(log_decay, axis=0)
    cum_t = cum_decay.T
    diff = cum_t[:, :, None] - cum_t[:, None, :]
    lower = (jnp.arange(tok_dev)[:, None] >= jnp.arange(tok_dev)[None, :])[None]
    decay_mask = jnp.where(lower, jnp.exp(jnp.where(lower, diff, 0.0)), 0.0)
    scores = (
        jnp.einsum("thd,shd->hts", queries, key_rows, preferred_element_type=jnp.float32)
        * decay_mask
    )
    tail = jnp.exp(cum_decay[-1][None, :] - cum_decay)
    lead_decay = jnp.exp(cum_decay)
    summary = jnp.einsum("shd,she->hde", key_f * tail[:, :, None], value_f, precision=hi)
    backsum = jnp.einsum("thd,the->hde", query_f * lead_decay[:, :, None], cot_f, precision=hi)
    zeros_state = jnp.zeros((heads_here, head_size, head_size), jnp.float32)
    block_decay = jnp.exp(cum_decay[-1])
    identity = (jnp.ones((heads_here,), jnp.float32), zeros_state)
    _, state_in = entering((block_decay, summary), "ctx", link, identity, False)
    _, grad_in = entering((block_decay, backsum), "ctx", link, identity, True)
    local = jnp.einsum("hts,shd->thd", scores, value_f, precision=hi)
    carried = jnp.einsum("thd,hde->the", query_f, state_in, precision=hi) * lead_decay[:, :, None]
    attended = local + carried
    dov = (
        jnp.einsum("thd,shd->hts", cot_rows, val_rows, preferred_element_type=jnp.float32)
        * decay_mask
    )
    grad_q = jnp.einsum("hts,shd->thd", dov, key_f, precision=hi)
    grad_q = grad_q + lead_decay[:, :, None] * jnp.einsum(
        "the,hde->thd", cot_f, state_in, precision=hi
    )
    grad_k = jnp.einsum("hts,thd->shd", dov, query_f, precision=hi)
    grad_k = grad_k + tail[:, :, None] * jnp.einsum("the,hde->thd", value_f, grad_in, precision=hi)
    grad_v = jnp.einsum("hts,the->she", scores, cot_f, precision=hi)
    grad_v = grad_v + tail[:, :, None] * jnp.einsum("thd,hde->the", key_f, grad_in, precision=hi)
    headed = rms_norm(attended, norm_gain.reshape(heads_here, head_size)).reshape(tok_dev, chans)
    headed = headed.astype(jnp.bfloat16)
    partial_out = jnp.dot(headed, w_out, preferred_element_type=jnp.float32)
    attn_total = lax.psum(partial_out.astype(jnp.bfloat16), "head").astype(jnp.float32)
    resid_full = x_float + attn_total
    moe_in = rms_norm(resid_full, gain_moe).astype(jnp.bfloat16)
    resid_mine = lax.dynamic_slice_in_dim(resid_full, my_head * cols, cols, 1)
    hot = (expert_ids[:, :, None] == jnp.arange(experts, dtype=jnp.int32)).astype(jnp.int32)
    counts = jnp.sum(hot, axis=1)
    ranks = jnp.cumsum(counts, axis=0) - counts
    slot = jnp.sum(hot * ranks[:, None, :], axis=-1)
    owner = expert_ids // EXP_CTX
    local_id = expert_ids % EXP_CTX
    picked = local_id == local_expert
    source_rows = jnp.broadcast_to(moe_in[:, None, :], (tok_dev, TOP, width)).reshape(-1, width)
    total = jnp.zeros((tok_dev, width), jnp.float32)
    positions = jnp.where(picked, owner * cap + slot, n_ctx * cap).reshape(-1)
    buffer = (
        jnp.zeros((n_ctx * cap, width), jnp.bfloat16).at[positions].set(source_rows, mode="drop")
    )
    buffer = buffer.reshape(n_ctx, cap, width)
    batch = lax.all_to_all(buffer, "ctx", split_axis=0, concat_axis=0, tiled=True)
    gate_val = jnp.einsum("ncd,df->ncf", batch, w_gate[0], preferred_element_type=jnp.float32)
    up_val = jnp.einsum("ncd,df->ncf", batch, w_up[0], preferred_element_type=jnp.float32)
    inner = (jax.nn.silu(gate_val) * up_val).astype(jnp.bfloat16)
    returned = lax.all_to_all(
        jnp.einsum("ncf,fd->ncd", inner, w_down[0], preferred_element_type=jnp.float32).astype(
            jnp.bfloat16
        ),
        "ctx",
        split_axis=0,
        concat_axis=0,
        tiled=True,
    )
    flat_back = returned.reshape(n_ctx * cap, width)
    fetch = jnp.where(picked, owner * cap + slot, 0)
    weights = jnp.where(picked, route_weights, 0.0)
    for chosen in range(TOP):
        total = total + weights[:, chosen, None] * flat_back[fetch[:, chosen]].astype(jnp.float32)
    moe_out = lax.psum_scatter(
        total.astype(jnp.bfloat16), "head", scatter_dimension=1, tiled=True
    ).astype(jnp.float32)
    layer_out = (resid_mine + moe_out).astype(jnp.bfloat16)
    return (
        layer_out,
        grad_q.reshape(tok_dev, chans).astype(jnp.bfloat16),
        grad_k.reshape(tok_dev, chans).astype(jnp.bfloat16),
        grad_v.reshape(tok_dev, chans).astype(jnp.bfloat16),
    )


def solution(mesh):
    in_specs = (
        P("ctx", None),
        P(),
        P(None, None, "head"),
        P(None, None, "head"),
        P("ctx", "head"),
        P("head"),
        P("head", None),
        P(),
        P("ctx", None),
        P("ctx", None),
        P(("ctx", "head"), None, None),
        P(("ctx", "head"), None, None),
        P(("ctx", "head"), None, None),
        P("ctx", "head"),
    )
    out_specs = (P("ctx", "head"), P("ctx", "head"), P("ctx", "head"), P("ctx", "head"))
    return jax.shard_map(body, mesh=mesh, in_specs=in_specs, out_specs=out_specs, check_vma=False)
```

profile of v0, /device:TPU:32, one launch (start us, length us, event | category | flops | bytes accessed | tf_op | source)
XLA Modules:
  0.0 524.5 jit_solution(18386399533522410628)
XLA Ops:
  7.2 1.7 fusion.6
  9.4 2.3 convolution_convert_fusion.2
  12.4 1.7 collective-permute-start
  15.5 1.1 maximum_convert_fusion
  18.4 25.0 %all-gather.2 = f32[32,1,2]{2,1,0:T(1,128)S(1)} all-gather(f32[1,1,2]{2,1,0:T(1,128)S(1)} %bitcast.218), channel_id=1, replica_groups=mesh['ctx'=32,'head'=8] {'ctx'}, dimensions={0}, use_global_device_ids=true | all-gather | bytes 264 | tf_op jit(solution)/shard_map/all_gather | solution.py:19
  45.1 29.0 %all-gather.6.cloned.1.call-done = f32[64,128,128]{2,1,0:T(8,128)} async-done(((f32[2,128,128]{2,1,0:T(8,128)}), f32[64,128,128]{2,1,0:T(8,128)}) %all-gather.6.cloned.1.call-update) | async-done | bytes 4194320 | tf_op jit(solution)/shard_map/all_gather | solution.py:19
  74.0 32.2 %while.28 = (s32[]{:T(128)}, f32[2,128,128]{2,1,0:T(8,128)S(1)}, s32[]{:T(128)}, f32[32,2]{1,0:T(8,128)S(1)}, f32[32,2,128,128]{3,2,1,0:T(8,128)}, /*index=5*/s32[]{:T(128)}, s32[]{:T(128)}) while((s32[]{:T(128)}, f32[2,128,128]{2,1,0:T(8,128)S(1)}, s32[]{:T(128)}, f32[32,2]{1,0:T(8,128)S(1)}, f32[32,2,128,128]{3,2,1,0:T(8,128)}, ...), condition=%wide.region_4.5_spmd.clone, body=%wide.region_3.4_spmd.clone.sunk | while | flops 131076 | bytes 393353 | solution.py:31
  74.0 1.1 fusion.86
  76.2 1.0 fusion.86
  77.2 1.0 fusion.86
  80.3 1.0 fusion.86
  83.5 1.0 fusion.86
  84.5 1.0 fusion.86
  87.6 1.0 fusion.86
  88.6 1.0 fusion.86
  91.8 1.0 fusion.86
  92.8 1.0 fusion.86
  95.9 1.0 fusion.86
  97.0 1.0 fusion.86
  100.1 1.0 fusion.86
  103.2 1.0 fusion.86
  107.3 1.4 convolution_convert_fusion.1
  110.4 73.6 %all-reduce.2.cloned.1.call-done = bf16[256,2048]{1,0:T(8,128)(2,1)} async-done(((bf16[256,2048]{1,0:T(8,128)(2,1)}), bf16[256,2048]{1,0:T(8,128)(2,1)}) %all-reduce.2.cloned.1.call-update) | async-done | bytes 1048592 | tf_op jit(solution)/shard_map/psum | solution.py:129
  184.0 3.0 convert_add_fusion
  187.5 16.4 %scatter_custom_fusion = bf16[1536,2048]{1,0:T(8,128)(2,1)} fusion(s32[2048]{0:T(1024)} %bitcast.196, bf16[256,2048]{1,0:T(8,128)(2,1)S(1)} %multiply_convert_fusion, bf16[]{:T(256)} %constant.131.clone.1), kind=kCustom, calls=%fused_computation.15 | custom fusion | bytes 7340544 | tf_op jit(solution)/shard_map/scatter | solution.py:144
  203.9 7.4 %all-to-all-start = ((bf16[32,48,2048]{2,1,0:T(8,128)(2,1)}), bf16[32,48,2048]{2,1,0:T(8,128)(2,1)}, u32[]{:S(2)}, u32[]{:S(2)}) async-start(bf16[32,48,2048]{2,1,0:T(8,128)(2,1)} %bitcast.179), calls=%async_computation | async-start | bytes 12582912 | tf_op jit(solution)/shard_map/all_to_all | solution.py:147
  212.5 81.7 %all-to-all-done = bf16[32,48,2048]{2,1,0:T(8,128)(2,1)} async-done(((bf16[32,48,2048]{2,1,0:T(8,128)(2,1)}), bf16[32,48,2048]{2,1,0:T(8,128)(2,1)}, u32[]{:S(2)}, u32[]{:S(2)}) %all-to-all-start) | async-done | bytes 6291488 | tf_op jit(solution)/shard_map/all_to_all | solution.py:147
  294.1 5.9 %fusion.26 = f32[32,48,256]{2,1,0:T(8,128)} fusion(bf16[32,48,2048]{2,1,0:T(8,128)(2,1)} %all-to-all-done, bf16[1,2048,256]{2,1,0:T(8,128)(2,1)S(1)} %copy-done.30), kind=kOutput, calls=%fused_computation.57 | convolution fusion | flops 1610612736 | bytes 8912896 | tf_op jit(solution)/shard_map/ncd,df->ncf/dot_general | solution.py:148
  300.1 12.6 %convolution_convert_fusion = bf16[32,48,2048]{2,1,0:T(8,128)(2,1)} fusion(f32[32,48,256]{2,1,0:T(8,128)} %fusion.26, bf16[32,48,2048]{2,1,0:T(8,128)(2,1)} %all-to-all-done, bf16[1,256,2048]{2,1,0:T(8,128)(2,1)S(1)} %copy-done.31, bf16[1,2048,256]{2,1,0:T(8,128)(2,1)} %param.29), kind=kOutput, calls=%fused_computation.17 | convolution fusion | flops 3226730496 | bytes 16252928 | tf_op jit(solution)/shard_map/ncf,fd->ncd/dot_general | solution.py:152
  312.7 5.0 all-to-all-start.1
  321.8 1.1 fusion.9
  322.9 4.6 rev.7
  327.5 68.1 %all-to-all-done.1 = bf16[32,48,2048]{2,1,0:T(8,128)(2,1)} async-done(((bf16[32,48,2048]{2,1,0:T(8,128)(2,1)}), bf16[32,48,2048]{2,1,0:T(8,128)(2,1)}, u32[]{:S(2)}, u32[]{:S(2)}) %all-to-all-start.1) | async-done | bytes 6291488 | tf_op jit(solution)/shard_map/all_to_all | solution.py:151
  395.6 6.0 %gather_fusion.7 = bf16[256,2048]{1,0:T(8,128)(2,1)S(1)} fusion(bf16[1536,2048]{1,0:T(8,128)(2,1)} %bitcast.21, s32[1024]{0:T(1024)S(1)} %pad_clamp_fusion), kind=kCustom, calls=%fused_computation.7 | custom fusion | bytes 2098176 | tf_op jit(solution)/shard_map/gather | solution.py:164
  401.6 6.0 %gather_fusion.6 = bf16[256,2048]{1,0:T(8,128)(2,1)S(1)} fusion(bf16[1536,2048]{1,0:T(8,128)(2,1)} %bitcast.21, s32[1024]{0:T(1024)S(1)} %pad_clamp_fusion.1), kind=kCustom, calls=%fused_computation.6 | custom fusion | bytes 2098176 | tf_op jit(solution)/shard_map/gather | solution.py:164
  407.6 6.0 %gather_fusion.5 = bf16[256,2048]{1,0:T(8,128)(2,1)S(1)} fusion(bf16[1536,2048]{1,0:T(8,128)(2,1)} %bitcast.21, s32[1024]{0:T(1024)S(1)} %pad_clamp_fusion.2), kind=kCustom, calls=%fused_computation.5 | custom fusion | bytes 2098176 | tf_op jit(solution)/shard_map/gather | solution.py:164
  413.5 7.1 %gather_fusion.4 = bf16[256,2048]{1,0:T(8,128)(2,1)} fusion(bf16[1536,2048]{1,0:T(8,128)(2,1)} %bitcast.21, s32[1024]{0:T(1024)} %pad_clamp_fusion.3), kind=kCustom, calls=%fused_computation.4 | custom fusion | bytes 2098176 | tf_op jit(solution)/shard_map/gather | solution.py:164
  420.6 7.3 %gather_fusion.3 = bf16[256,2048]{1,0:T(8,128)(2,1)} fusion(bf16[1536,2048]{1,0:T(8,128)(2,1)} %bitcast.21, s32[1024]{0:T(1024)} %pad_clamp_fusion.4), kind=kCustom, calls=%fused_computation.3 | custom fusion | bytes 2098176 | tf_op jit(solution)/shard_map/gather | solution.py:164
  427.9 7.1 %gather_fusion.2 = bf16[256,2048]{1,0:T(8,128)(2,1)} fusion(bf16[1536,2048]{1,0:T(8,128)(2,1)} %bitcast.21, s32[1024]{0:T(1024)} %pad_clamp_fusion.5), kind=kCustom, calls=%fused_computation.2 | custom fusion | bytes 2098176 | tf_op jit(solution)/shard_map/gather | solution.py:164
  435.0 7.1 %gather_fusion.1 = bf16[256,2048]{1,0:T(8,128)(2,1)} fusion(bf16[1536,2048]{1,0:T(8,128)(2,1)} %bitcast.21, s32[1024]{0:T(1024)} %pad_clamp_fusion.6), kind=kCustom, calls=%fused_computation.1 | custom fusion | bytes 2098176 | tf_op jit(solution)/shard_map/gather | solution.py:164
  442.0 7.0 %gather_fusion = bf16[256,2048]{1,0:T(8,128)(2,1)} fusion(bf16[1536,2048]{1,0:T(8,128)(2,1)} %bitcast.21, s32[1024]{0:T(1024)S(1)} %pad_clamp_fusion.7), kind=kCustom, calls=%fused_computation | custom fusion | bytes 2098176 | tf_op jit(solution)/shard_map/gather | solution.py:164
  449.0 4.6 add_convert_fusion
  453.7 52.9 %while.29 = (s32[]{:T(128)}, f32[2,128,128]{2,1,0:T(8,128)S(1)}, s32[]{:T(128)}, f32[32,2]{1,0:T(8,128)}, f32[32,2,128,128]{3,2,1,0:T(8,128)}, /*index=5*/s32[]{:T(128)}, s32[]{:T(128)}) while((s32[]{:T(128)}, f32[2,128,128]{2,1,0:T(8,128)S(1)}, s32[]{:T(128)}, f32[32,2]{1,0:T(8,128)}, f32[32,2,128,128]{3,2,1,0:T(8,128)}, ...), condition=%wide.region_15.16_spmd.clone, body=%wide.region_14.15_spmd.clone.sunk | while | flops 131076 | bytes 393353 | solution.py:31
  508.0 1.8 copy.199
  509.8 1.2 fusion.16
  511.0 1.5 fusion.18
  513.6 1.5 fusion.19
  515.8 1.7 add_convert_fusion.1
  (251 shorter events, 86.6 us)
Async XLA Ops:
  7.2 2.2 copy-start
  7.2 66.8 %all-gather.6.cloned.1.call-start = ((), (), s32[]{:S(2)}) async-start(), calls=%async_computation.5 | async-start | bytes 4325376 | tf_op jit(solution)/shard_map/all_gather | solution.py:19
  9.4 4.8 copy-start.28
  9.4 6.0 %copy-start.19 = (f32[4,3,256]{2,0,1:T(4,128)S(1)}, f32[4,3,256]{2,0,1:T(4,128)}, u32[]{:S(2)}) copy-start(f32[4,3,256]{2,0,1:T(4,128)} %param.21) | copy-start | bytes 36868
  11.7 0.7 copy-start.13
  12.4 3.1 collective-permute-start
  15.2 29.5 %copy-start.25 = (f32[1,2,2,128]{3,1,2,0:T(2,128)}, f32[1,2,2,128]{3,1,2,0:T(2,128)S(1)}, u32[]{:S(2)}) copy-start(f32[1,2,2,128]{3,1,2,0:T(2,128)S(1)} %copy.239) | copy-start | bytes 6148
  16.6 27.0 %copy-start.14 = (s32[256,8]{0,1:T(8,128)S(1)}, s32[256,8]{0,1:T(8,128)}, u32[]{:S(2)}) copy-start(s32[256,8]{0,1:T(8,128)} %param.26) | copy-start | bytes 24580
  17.2 56.8 %copy-start.9 = (bf16[256,2,128]{2,1,0:T(2,128)(2,1)}, bf16[256,2,128]{2,1,0:T(2,128)(2,1)S(1)}, u32[]{:S(2)}) copy-start(bf16[256,2,128]{2,1,0:T(2,128)(2,1)S(1)} %convert_element_type.119) | copy-start | bytes 393220
  17.4 27.2 %copy-start.11 = (bf16[256,2,128]{0,2,1:T(8,128)(2,1)}, bf16[256,2,128]{0,2,1:T(8,128)(2,1)S(1)}, u32[]{:S(2)}) copy-start(bf16[256,2,128]{0,2,1:T(8,128)(2,1)S(1)} %copy.176) | copy-start | bytes 393220
  18.3 165.6 %all-reduce.2.cloned.1.call-start = ((), (), s32[]{:S(2)}) async-start(), calls=%async_computation.3 | async-start | bytes 2097152 | tf_op jit(solution)/shard_map/psum | solution.py:129
  43.5 30.5 %copy-start.20 = (f32[32,1,2]{0,2,1:T(2,128)}, f32[32,1,2]{0,2,1:T(2,128)S(1)}, u32[]{:S(2)}) copy-start(f32[32,1,2]{0,2,1:T(2,128)S(1)} %copy.175) | copy-start | bytes 772
  44.5 62.1 %copy-start.24 = (s32[64,3]{0,1:T(4,128)}, s32[64,3]{0,1:T(4,128)S(1)}, u32[]{:S(2)}) copy-start(s32[64,3]{0,1:T(4,128)S(1)} %reduce-window.19) | copy-start | bytes 2308
  44.6 62.0 %copy-start.16 = (pred[256,256]{1,0:T(8,128)(4,1)}, pred[256,256]{1,0:T(8,128)(4,1)S(1)}, u32[]{:S(2)}) copy-start(pred[256,256]{1,0:T(8,128)(4,1)S(1)} %iota_compare_fusion.1) | copy-start | bytes 196612
  44.7 166.8 %copy-start.6 = (bf16[256,1,256]{0,2,1:T(8,128)(2,1)}, bf16[256,1,256]{0,2,1:T(8,128)(2,1)S(1)}, u32[]{:S(2)}) copy-start(bf16[256,1,256]{0,2,1:T(8,128)(2,1)S(1)} %copy.207) | copy-start | bytes 393220
  45.0 62.1 %copy-start.4 = (f32[2,256,256]{2,1,0:T(8,128)}, f32[2,256,256]{2,1,0:T(8,128)S(1)}, u32[]{:S(2)}) copy-start(f32[2,256,256]{2,1,0:T(8,128)S(1)} %convolution_multiply_fusion) | copy-start | bytes 1572868
  45.0 62.1 %copy-start.29 = (f32[256]{0:T(256)S(1)}, f32[256]{0:T(256)}, u32[]{:S(2)}) copy-start(f32[256]{0:T(256)} %param.23) | copy-start | bytes 3076
  74.0 33.2 %copy-start.12 = (bf16[256,2048]{1,0:T(8,128)(2,1)S(1)}, bf16[256,2048]{1,0:T(8,128)(2,1)}, u32[]{:S(2)}) copy-start(bf16[256,2048]{1,0:T(8,128)(2,1)} %param.24) | copy-start | bytes 3145732
  107.1 1.7 slice-start
  107.1 1.8 copy-start.23
  107.1 76.9 %copy-start.2 = (bf16[256,2048]{1,0:T(8,128)(2,1)S(1)}, bf16[256,2048]{1,0:T(8,128)(2,1)}, u32[]{:S(2)}) copy-start(bf16[256,2048]{1,0:T(8,128)(2,1)} %param.18) | copy-start | bytes 3145732
  184.0 3.0 copy-start.3
  184.0 3.0 copy-start.22
  203.9 7.4 %copy-start.15 = (bf16[256,256]{1,0:T(8,128)(2,1)S(1)}, bf16[256,256]{1,0:T(8,128)(2,1)}, u32[]{:S(2)}) copy-start(bf16[256,256]{1,0:T(8,128)(2,1)} %param.31) | copy-start | bytes 393220
  203.9 90.2 %copy-start.30 = (bf16[1,2048,256]{2,1,0:T(8,128)(2,1)S(1)}, bf16[1,2048,256]{2,1,0:T(8,128)(2,1)}, u32[]{:S(2)}) copy-start(bf16[1,2048,256]{2,1,0:T(8,128)(2,1)} %param.28) | copy-start | bytes 3145732
  203.9 90.2 %all-to-all-start = ((bf16[32,48,2048]{2,1,0:T(8,128)(2,1)}), bf16[32,48,2048]{2,1,0:T(8,128)(2,1)}, u32[]{:S(2)}, u32[]{:S(2)}) async-start(bf16[32,48,2048]{2,1,0:T(8,128)(2,1)} %bitcast.179), calls=%async_computation | async-start | bytes 12582912 | tf_op jit(solution)/shard_map/all_to_all | solution.py:147
  211.3 111.6 %all-gather.8.cloned.1.call-start = ((), (), s32[]{:S(2)}) async-start(), calls=%async_computation.6 | async-start | bytes 4325376 | tf_op jit(solution)/shard_map/all_gather | solution.py:19
  211.5 110.4 %copy-start.7 = (bf16[256,256]{0,1:T(8,128)(2,1)}, bf16[256,256]{0,1:T(8,128)(2,1)S(1)}, u32[]{:S(2)}) copy-start(bf16[256,256]{0,1:T(8,128)(2,1)S(1)} %copy.208) | copy-start | bytes 393220
  212.4 87.6 %copy-start.31 = (bf16[1,256,2048]{2,1,0:T(8,128)(2,1)S(1)}, bf16[1,256,2048]{2,1,0:T(8,128)(2,1)}, u32[]{:S(2)}) copy-start(bf16[1,256,2048]{2,1,0:T(8,128)(2,1)} %param.30) | copy-start | bytes 3145732
  312.7 5.3 %copy-start.21 = (f32[32,1,2]{0,2,1:T(2,128)S(1)}, f32[32,1,2]{0,2,1:T(2,128)}, u32[]{:S(2)}) copy-start(f32[32,1,2]{0,2,1:T(2,128)} %copy-done.20) | copy-start | bytes 772
  312.7 8.5 %copy-start.18 = (f32[256,8]{0,1:T(8,128)S(1)}, f32[256,8]{0,1:T(8,128)}, u32[]{:S(2)}) copy-start(f32[256,8]{0,1:T(8,128)} %get-tuple-element.336) | copy-start | bytes 24580
  312.7 9.1 %copy-start.17 = (pred[256,256]{1,0:T(8,128)(4,1)S(1)}, pred[256,256]{1,0:T(8,128)(4,1)}, u32[]{:S(2)}) copy-start(pred[256,256]{1,0:T(8,128)(4,1)} %copy-done.16) | copy-start | bytes 196612
  312.7 9.1 %copy-start.26 = (f32[1,2,2,128]{3,1,2,0:T(2,128)S(1)}, f32[1,2,2,128]{3,1,2,0:T(2,128)}, u32[]{:S(2)}) copy-start(f32[1,2,2,128]{3,1,2,0:T(2,128)} %copy-done.25) | copy-start | bytes 6148
  312.7 83.0 %all-to-all-start.1 = ((bf16[32,48,2048]{2,1,0:T(8,128)(2,1)}), bf16[32,48,2048]{2,1,0:T(8,128)(2,1)}, u32[]{:S(2)}, u32[]{:S(2)}) async-start(bf16[32,48,2048]{2,1,0:T(8,128)(2,1)} %convolution_convert_fusion), calls=%async_computation.1 | async-start | bytes 12582912 | tf_op jit(solution)/shard_map/all_to_all | solution.py:151
  317.7 198.0 %reduce-scatter.2.cloned.1.call-start = ((), (), s32[]{:S(2)}) async-start(), calls=%async_computation.4 | async-start | bytes 1179648 | tf_op jit(solution)/shard_map/reduce_scatter | solution.py:165
  442.0 7.0 %copy-start.27 = (f32[256,1]{0,1:T(1,128)S(1)}, f32[256,1]{0,1:T(1,128)}, u32[]{:S(2)}) copy-start(f32[256,1]{0,1:T(1,128)} %get-tuple-element.350) | copy-start | bytes 3076
  453.6 53.0 %copy-start.10 = (bf16[256,2,128]{2,1,0:T(2,128)(2,1)S(1)}, bf16[256,2,128]{2,1,0:T(2,128)(2,1)}, u32[]{:S(2)}) copy-start(bf16[256,2,128]{2,1,0:T(2,128)(2,1)} %copy-done.9) | copy-start | bytes 393220
  453.6 53.3 %copy-start.5 = (f32[2,256,256]{2,1,0:T(8,128)S(1)}, f32[2,256,256]{2,1,0:T(8,128)}, u32[]{:S(2)}) copy-start(f32[2,256,256]{2,1,0:T(8,128)} %copy-done.4) | copy-start | bytes 1572868
  453.6 53.3 %copy-start.8 = (bf16[256,256]{0,1:T(8,128)(2,1)S(1)}, bf16[256,256]{0,1:T(8,128)(2,1)}, u32[]{:S(2)}) copy-start(bf16[256,256]{0,1:T(8,128)(2,1)} %copy-done.7) | copy-start | bytes 393220
  508.0 9.5 %copy-start.1 = (bf16[2048,3,256]{2,0,1:T(8,128)(2,1)S(1)}, bf16[2048,3,256]{2,0,1:T(8,128)(2,1)}, u32[]{:S(2)}) copy-start(bf16[2048,3,256]{2,0,1:T(8,128)(2,1)} %param.20) | copy-start | bytes 9437188
Sparse Core Ops, SparseCore 0:
  18.5 55.5 all-gather.5
  108.9 75.0 all-reduce.1
  215.3 86.4 all-gather.7
  453.8 31.1 reduce-scatter.1
where the time goes:
time: 535 us; the launch traced here: 524 us
  waiting for transfers between devices  252 us (47%)
  local copies, waits for them, and re-layouts  104 us (19%)
  other arithmetic  80.3 us (15%)
  matrix products  32 us (6%)
  blocking collectives  25 us (5%)
  between operations  14.9 us (3%)
  starting transfers between devices  14.4 us (3%)
    all_to_all x1, waiting for transfers between devices, body(): lax.all_to_all(buffer, 'ctx', split_axis=0, concat_axis=0, tiled=True)  81.7 us
    psum x1, waiting for transfers between devices, body(): lax.psum(partial_out.astype(jnp.bfloat16), 'head').astype(jnp.float32)  73.6 us
    all_to_all x1, waiting for transfers between devices, body(): lax.all_to_all(jnp.einsum('ncf,fd->ncd', inner, w_down[0], preferred_elem...  68.1 us
    select_n x62, other arithmetic, hop(): jnp.where(position < mine, new, old)  61.6 us
    gather x8, local copies, waits for them, and re-layouts, body(): flat_back[fetch[:, chosen]].astype(jnp.float32)  53.3 us
    all_gather x2, waiting for transfers between devices, entering(): pieces = jax.tree.map(lambda part: lax.all_gather(part, axis), value)  29 us
    all_gather x1, blocking collectives, entering(): pieces = jax.tree.map(lambda part: lax.all_gather(part, axis), value)  25 us
    mul x62, local copies, waits for them, and re-layouts, link(): later[0][:, None, None] * earlier[1] + later[1]  21.8 us
  transfers between devices with their start and end apart: 7, of which 4 were waited for; matrix products, arithmetic and copies ran while one was open for 18% of the time, Pallas kernels for 0%

commit v1 on v0

--- a/solution.py
+++ b/solution.py
@@ -55,6 +55,10 @@
     w_down,
     grad_core,
 ):
+
+    def skins_note(u):
+        return jnp.sum(lax.all_gather(u, "head"), 0)
+
     hi = lax.Precision.HIGHEST
     n_ctx = lax.axis_size("ctx")
     n_head = lax.axis_size("head")
@@ -126,7 +130,7 @@
     headed = rms_norm(attended, norm_gain.reshape(heads_here, head_size)).reshape(tok_dev, chans)
     headed = headed.astype(jnp.bfloat16)
     partial_out = jnp.dot(headed, w_out, preferred_element_type=jnp.float32)
-    attn_total = lax.psum(partial_out.astype(jnp.bfloat16), "head").astype(jnp.float32)
+    attn_total = skins_note(partial_out.astype(jnp.bfloat16)).astype(jnp.float32)
     resid_full = x_float + attn_total
     moe_in = rms_norm(resid_full, gain_moe).astype(jnp.bfloat16)
     resid_mine = lax.dynamic_slice_in_dim(resid_full, my_head * cols, cols, 1)

time: 535 us -> 551 us (1.030)
  waiting for transfers between devices: 252 us -> 266 us
    all_gather x0 -> x1, waiting for transfers between devices: none -> 89.3 us  [skins_note(): return jnp.sum(lax.all_gather(u, 'head'), 0)]
    psum x1 -> x0, waiting for transfers between devices: 73.6 us -> none  [body(): lax.psum(partial_out.astype(jnp.bfloat16), 'head').astype(jnp.float32)]
  transfers between devices with their start and end apart: 7 -> 7, of which waited for: 4 -> 4; matrix products, arithmetic and copies ran while one was open for 18% -> 17% of each run, Pallas kernels for 0% -> 0%
where the time goes in v1:
time: 551 us; the launch traced here: 543 us
  waiting for transfers between devices  266 us (48%)
  local copies, waits for them, and re-layouts  104 us (19%)
  other arithmetic  84.3 us (15%)
  matrix products  32.4 us (6%)
  blocking collectives  25.6 us (5%)
  between operations  14.9 us (3%)
  starting transfers between devices  14.7 us (3%)
    all_gather x1, waiting for transfers between devices, skins_note(): return jnp.sum(lax.all_gather(u, 'head'), 0)  89.3 us
    all_to_all x1, waiting for transfers between devices, body(): lax.all_to_all(buffer, 'ctx', split_axis=0, concat_axis=0, tiled=True)  79.4 us
    all_to_all x1, waiting for transfers between devices, body(): lax.all_to_all(jnp.einsum('ncf,fd->ncd', inner, w_down[0], preferred_elem...  68 us
    select_n x62, other arithmetic, hop(): jnp.where(position < mine, new, old)  61.6 us
    gather x8, local copies, waits for them, and re-layouts, body(): flat_back[fetch[:, chosen]].astype(jnp.float32)  53.4 us
    all_gather x2, waiting for transfers between devices, entering(): pieces = jax.tree.map(lambda part: lax.all_gather(part, axis), value)  28.8 us
    all_gather x1, blocking collectives, entering(): pieces = jax.tree.map(lambda part: lax.all_gather(part, axis), value)  25.6 us
    mul x62, local copies, waits for them, and re-layouts, link(): later[0][:, None, None] * earlier[1] + later[1]  21.7 us
  transfers between devices with their start and end apart: 7, of which 4 were waited for; matrix products, arithmetic and copies ran while one was open for 17% of the time, Pallas kernels for 0%

profile of v1, /device:TPU:32, one launch (start us, length us, event | category | flops | bytes accessed | tf_op | source)
XLA Modules:
  0.0 542.9 jit_solution(14343354105941075919)
XLA Ops:
  7.2 1.7 fusion.6
  9.4 2.3 convolution_convert_fusion.2
  12.4 1.7 collective-permute-start
  15.5 1.1 maximum_convert_fusion
  18.4 25.6 %all-gather.3 = f32[32,1,2]{2,1,0:T(1,128)S(1)} all-gather(f32[1,1,2]{2,1,0:T(1,128)S(1)} %bitcast.220), channel_id=1, replica_groups=mesh['ctx'=32,'head'=8] {'ctx'}, dimensions={0}, use_global_device_ids=true | all-gather | bytes 264 | tf_op jit(solution)/shard_map/all_gather | solution.py:19
  45.2 28.7 %all-gather.8.cloned.1.call-done = f32[64,128,128]{2,1,0:T(8,128)} async-done(((f32[2,128,128]{2,1,0:T(8,128)}), f32[64,128,128]{2,1,0:T(8,128)}) %all-gather.8.cloned.1.call-update) | async-done | bytes 4194320 | tf_op jit(solution)/shard_map/all_gather | solution.py:19
  74.0 32.2 %while.28 = (s32[]{:T(128)}, f32[2,128,128]{2,1,0:T(8,128)S(1)}, s32[]{:T(128)}, f32[32,2]{1,0:T(8,128)S(1)}, f32[32,2,128,128]{3,2,1,0:T(8,128)}, /*index=5*/s32[]{:T(128)}, s32[]{:T(128)}) while((s32[]{:T(128)}, f32[2,128,128]{2,1,0:T(8,128)S(1)}, s32[]{:T(128)}, f32[32,2]{1,0:T(8,128)S(1)}, f32[32,2,128,128]{3,2,1,0:T(8,128)}, ...), condition=%wide.region_4.5_spmd.clone, body=%wide.region_3.4_spmd.clone.sunk | while | flops 131076 | bytes 393353 | solution.py:31
  74.0 1.1 fusion.86
  75.1 1.0 fusion.86
  76.2 1.0 fusion.86
  79.3 1.0 fusion.86
  80.3 1.0 fusion.86
  83.4 1.0 fusion.86
  84.5 1.0 fusion.86
  87.6 1.0 fusion.86
  88.6 1.0 fusion.86
  91.7 1.0 fusion.86
  94.8 1.0 fusion.86
  95.9 1.0 fusion.86
  107.2 1.5 convolution_convert_fusion.1
  111.3 89.3 %all-gather.10.cloned.1.call-done = bf16[2048,2048]{1,0:T(8,128)(2,1)} async-done(((bf16[256,2048]{1,0:T(8,128)(2,1)}), bf16[2048,2048]{1,0:T(8,128)(2,1)}) %all-gather.10.cloned.1.call-update) | async-done | bytes 8388624 | tf_op jit(solution)/shard_map/all_gather | solution.py:60
  200.7 5.3 reduce_sum.59
  206.0 1.7 convert_add_fusion
  208.2 15.9 %scatter_custom_fusion = bf16[1536,2048]{1,0:T(8,128)(2,1)} fusion(s32[2048]{0:T(1024)} %bitcast.198, bf16[256,2048]{1,0:T(8,128)(2,1)S(1)} %multiply_convert_fusion, bf16[]{:T(256)} %constant.125.clone.1), kind=kCustom, calls=%fused_computation.15 | custom fusion | bytes 7340544 | tf_op jit(solution)/shard_map/scatter | solution.py:148
  224.1 7.3 %all-to-all-start = ((bf16[32,48,2048]{2,1,0:T(8,128)(2,1)}), bf16[32,48,2048]{2,1,0:T(8,128)(2,1)}, u32[]{:S(2)}, u32[]{:S(2)}) async-start(bf16[32,48,2048]{2,1,0:T(8,128)(2,1)} %bitcast.180), calls=%async_computation | async-start | bytes 12582912 | tf_op jit(solution)/shard_map/all_to_all | solution.py:151
  232.8 79.4 %all-to-all-done = bf16[32,48,2048]{2,1,0:T(8,128)(2,1)} async-done(((bf16[32,48,2048]{2,1,0:T(8,128)(2,1)}), bf16[32,48,2048]{2,1,0:T(8,128)(2,1)}, u32[]{:S(2)}, u32[]{:S(2)}) %all-to-all-start) | async-done | bytes 6291488 | tf_op jit(solution)/shard_map/all_to_all | solution.py:151
  312.2 6.0 %fusion.26 = f32[32,48,256]{2,1,0:T(8,128)} fusion(bf16[32,48,2048]{2,1,0:T(8,128)(2,1)} %all-to-all-done, bf16[1,2048,256]{2,1,0:T(8,128)(2,1)S(1)} %copy-done.28), kind=kOutput, calls=%fused_computation.57 | convolution fusion | flops 1610612736 | bytes 8912896 | tf_op jit(solution)/shard_map/ncd,df->ncf/dot_general | solution.py:152
  318.2 12.8 %convolution_convert_fusion = bf16[32,48,2048]{2,1,0:T(8,128)(2,1)} fusion(f32[32,48,256]{2,1,0:T(8,128)} %fusion.26, bf16[32,48,2048]{2,1,0:T(8,128)(2,1)} %all-to-all-done, bf16[1,256,2048]{2,1,0:T(8,128)(2,1)S(1)} %copy-done.29, bf16[1,2048,256]{2,1,0:T(8,128)(2,1)} %param.29), kind=kOutput, calls=%fused_computation.17 | convolution fusion | flops 3226730496 | bytes 16252928 | tf_op jit(solution)/shard_map/ncf,fd->ncd/dot_general | solution.py:156
  331.0 5.0 all-to-all-start.1
  340.2 1.1 fusion.9
  341.3 4.6 rev.7
  345.9 68.0 %all-to-all-done.1 = bf16[32,48,2048]{2,1,0:T(8,128)(2,1)} async-done(((bf16[32,48,2048]{2,1,0:T(8,128)(2,1)}), bf16[32,48,2048]{2,1,0:T(8,128)(2,1)}, u32[]{:S(2)}, u32[]{:S(2)}) %all-to-all-start.1) | async-done | bytes 6291488 | tf_op jit(solution)/shard_map/all_to_all | solution.py:155
  414.0 6.0 %gather_fusion.7 = bf16[256,2048]{1,0:T(8,128)(2,1)S(1)} fusion(bf16[1536,2048]{1,0:T(8,128)(2,1)} %bitcast.22, s32[1024]{0:T(1024)S(1)} %pad_clamp_fusion), kind=kCustom, calls=%fused_computation.7 | custom fusion | bytes 2098176 | tf_op jit(solution)/shard_map/gather | solution.py:168
  419.9 6.0 %gather_fusion.6 = bf16[256,2048]{1,0:T(8,128)(2,1)S(1)} fusion(bf16[1536,2048]{1,0:T(8,128)(2,1)} %bitcast.22, s32[1024]{0:T(1024)S(1)} %pad_clamp_fusion.1), kind=kCustom, calls=%fused_computation.6 | custom fusion | bytes 2098176 | tf_op jit(solution)/shard_map/gather | solution.py:168
  425.9 6.0 %gather_fusion.5 = bf16[256,2048]{1,0:T(8,128)(2,1)S(1)} fusion(bf16[1536,2048]{1,0:T(8,128)(2,1)} %bitcast.22, s32[1024]{0:T(1024)S(1)} %pad_clamp_fusion.2), kind=kCustom, calls=%fused_computation.5 | custom fusion | bytes 2098176 | tf_op jit(solution)/shard_map/gather | solution.py:168
  431.9 7.1 %gather_fusion.4 = bf16[256,2048]{1,0:T(8,128)(2,1)} fusion(bf16[1536,2048]{1,0:T(8,128)(2,1)} %bitcast.22, s32[1024]{0:T(1024)} %pad_clamp_fusion.3), kind=kCustom, calls=%fused_computation.4 | custom fusion | bytes 2098176 | tf_op jit(solution)/shard_map/gather | solution.py:168
  439.0 7.3 %gather_fusion.3 = bf16[256,2048]{1,0:T(8,128)(2,1)} fusion(bf16[1536,2048]{1,0:T(8,128)(2,1)} %bitcast.22, s32[1024]{0:T(1024)} %pad_clamp_fusion.4), kind=kCustom, calls=%fused_computation.3 | custom fusion | bytes 2098176 | tf_op jit(solution)/shard_map/gather | solution.py:168
  446.3 7.1 %gather_fusion.2 = bf16[256,2048]{1,0:T(8,128)(2,1)} fusion(bf16[1536,2048]{1,0:T(8,128)(2,1)} %bitcast.22, s32[1024]{0:T(1024)} %pad_clamp_fusion.5), kind=kCustom, calls=%fused_computation.2 | custom fusion | bytes 2098176 | tf_op jit(solution)/shard_map/gather | solution.py:168
  453.4 7.1 %gather_fusion.1 = bf16[256,2048]{1,0:T(8,128)(2,1)} fusion(bf16[1536,2048]{1,0:T(8,128)(2,1)} %bitcast.22, s32[1024]{0:T(1024)} %pad_clamp_fusion.6), kind=kCustom, calls=%fused_computation.1 | custom fusion | bytes 2098176 | tf_op jit(solution)/shard_map/gather | solution.py:168
  460.4 7.0 %gather_fusion = bf16[256,2048]{1,0:T(8,128)(2,1)} fusion(bf16[1536,2048]{1,0:T(8,128)(2,1)} %bitcast.22, s32[1024]{0:T(1024)S(1)} %pad_clamp_fusion.7), kind=kCustom, calls=%fused_computation | custom fusion | bytes 2098176 | tf_op jit(solution)/shard_map/gather | solution.py:168
  467.4 4.7 add_convert_fusion
  472.1 52.9 %while.29 = (s32[]{:T(128)}, f32[2,128,128]{2,1,0:T(8,128)S(1)}, s32[]{:T(128)}, f32[32,2]{1,0:T(8,128)}, f32[32,2,128,128]{3,2,1,0:T(8,128)}, /*index=5*/s32[]{:T(128)}, s32[]{:T(128)}) while((s32[]{:T(128)}, f32[2,128,128]{2,1,0:T(8,128)S(1)}, s32[]{:T(128)}, f32[32,2]{1,0:T(8,128)}, f32[32,2,128,128]{3,2,1,0:T(8,128)}, ...), condition=%wide.region_15.16_spmd.clone, body=%wide.region_14.15_spmd.clone.sunk | while | flops 131076 | bytes 393353 | solution.py:31
  525.3 1.0 fusion.20
  526.3 1.8 copy.199
  528.2 1.2 fusion.16
  529.3 1.5 fusion.18
  531.9 1.5 fusion.19
  534.2 1.7 add_convert_fusion.1
  (247 shorter events, 88.3 us)
Async XLA Ops:
  7.2 2.2 copy-start
  7.2 66.8 %all-gather.8.cloned.1.call-start = ((), (), s32[]{:S(2)}) async-start(), calls=%async_computation.4 | async-start | bytes 4325376 | tf_op jit(solution)/shard_map/all_gather | solution.py:19
  9.4 4.8 copy-start.26
  9.4 6.0 %copy-start.18 = (f32[4,3,256]{2,0,1:T(4,128)S(1)}, f32[4,3,256]{2,0,1:T(4,128)}, u32[]{:S(2)}) copy-start(f32[4,3,256]{2,0,1:T(4,128)} %param.21) | copy-start | bytes 36868
  11.7 0.7 copy-start.12
  12.4 3.1 collective-permute-start
  15.2 29.7 %copy-start.23 = (f32[1,2,2,128]{3,1,2,0:T(2,128)}, f32[1,2,2,128]{3,1,2,0:T(2,128)S(1)}, u32[]{:S(2)}) copy-start(f32[1,2,2,128]{3,1,2,0:T(2,128)S(1)} %copy.239) | copy-start | bytes 6148
  17.2 56.7 %copy-start.8 = (bf16[256,2,128]{2,1,0:T(2,128)(2,1)}, bf16[256,2,128]{2,1,0:T(2,128)(2,1)S(1)}, u32[]{:S(2)}) copy-start(bf16[256,2,128]{2,1,0:T(2,128)(2,1)S(1)} %convert_element_type.121) | copy-start | bytes 393220
  17.4 27.4 %copy-start.10 = (bf16[256,2,128]{0,2,1:T(8,128)(2,1)}, bf16[256,2,128]{0,2,1:T(8,128)(2,1)S(1)}, u32[]{:S(2)}) copy-start(bf16[256,2,128]{0,2,1:T(8,128)(2,1)S(1)} %copy.176) | copy-start | bytes 393220
  18.3 182.4 %all-gather.10.cloned.1.call-start = ((), (), s32[]{:S(2)}) async-start(), calls=%async_computation.5 | async-start | bytes 9437184 | tf_op jit(solution)/shard_map/all_gather | solution.py:60
  44.0 0.6 copy-start.19
  44.7 29.3 %copy-start.15 = (pred[256,256]{1,0:T(8,128)(4,1)}, pred[256,256]{1,0:T(8,128)(4,1)S(1)}, u32[]{:S(2)}) copy-start(pred[256,256]{1,0:T(8,128)(4,1)S(1)} %iota_compare_fusion.1) | copy-start | bytes 196612
  44.9 187.0 %copy-start.5 = (bf16[256,1,256]{0,2,1:T(8,128)(2,1)}, bf16[256,1,256]{0,2,1:T(8,128)(2,1)S(1)}, u32[]{:S(2)}) copy-start(bf16[256,1,256]{0,2,1:T(8,128)(2,1)S(1)} %copy.207) | copy-start | bytes 393220
  45.2 62.0 %copy-start.3 = (f32[2,256,256]{2,1,0:T(8,128)}, f32[2,256,256]{2,1,0:T(8,128)S(1)}, u32[]{:S(2)}) copy-start(f32[2,256,256]{2,1,0:T(8,128)S(1)} %convolution_multiply_fusion) | copy-start | bytes 1572868
  45.2 61.8 %copy-start.27 = (f32[256]{0:T(256)S(1)}, f32[256]{0:T(256)}, u32[]{:S(2)}) copy-start(f32[256]{0:T(256)} %param.23) | copy-start | bytes 3076
  74.0 33.2 %copy-start.11 = (bf16[256,2048]{1,0:T(8,128)(2,1)S(1)}, bf16[256,2048]{1,0:T(8,128)(2,1)}, u32[]{:S(2)}) copy-start(bf16[256,2048]{1,0:T(8,128)(2,1)} %param.24) | copy-start | bytes 3145732
  107.0 1.7 copy-start.13
  107.2 2.7 copy-start.22
  200.7 5.3 copy-start.2
  206.0 1.7 copy-start.21
  224.1 7.6 %copy-start.14 = (bf16[256,256]{1,0:T(8,128)(2,1)S(1)}, bf16[256,256]{1,0:T(8,128)(2,1)}, u32[]{:S(2)}) copy-start(bf16[256,256]{1,0:T(8,128)(2,1)} %param.31) | copy-start | bytes 393220
  224.1 88.1 %copy-start.28 = (bf16[1,2048,256]{2,1,0:T(8,128)(2,1)S(1)}, bf16[1,2048,256]{2,1,0:T(8,128)(2,1)}, u32[]{:S(2)}) copy-start(bf16[1,2048,256]{2,1,0:T(8,128)(2,1)} %param.28) | copy-start | bytes 3145732
  224.1 88.1 %all-to-all-start = ((bf16[32,48,2048]{2,1,0:T(8,128)(2,1)}), bf16[32,48,2048]{2,1,0:T(8,128)(2,1)}, u32[]{:S(2)}, u32[]{:S(2)}) async-start(bf16[32,48,2048]{2,1,0:T(8,128)(2,1)} %bitcast.180), calls=%async_computation | async-start | bytes 12582912 | tf_op jit(solution)/shard_map/all_to_all | solution.py:151
  231.5 109.8 %all-gather.12.cloned.1.call-start = ((), (), s32[]{:S(2)}) async-start(), calls=%async_computation.6 | async-start | bytes 4325376 | tf_op jit(solution)/shard_map/all_gather | solution.py:19
  231.8 108.4 %copy-start.6 = (bf16[256,256]{0,1:T(8,128)(2,1)}, bf16[256,256]{0,1:T(8,128)(2,1)S(1)}, u32[]{:S(2)}) copy-start(bf16[256,256]{0,1:T(8,128)(2,1)S(1)} %copy.208) | copy-start | bytes 393220
  232.8 85.4 %copy-start.29 = (bf16[1,256,2048]{2,1,0:T(8,128)(2,1)S(1)}, bf16[1,256,2048]{2,1,0:T(8,128)(2,1)}, u32[]{:S(2)}) copy-start(bf16[1,256,2048]{2,1,0:T(8,128)(2,1)} %param.30) | copy-start | bytes 3145732
  331.0 5.3 copy-start.20
  331.0 8.6 %copy-start.17 = (f32[256,8]{0,1:T(8,128)S(1)}, f32[256,8]{0,1:T(8,128)}, u32[]{:S(2)}) copy-start(f32[256,8]{0,1:T(8,128)} %get-tuple-element.336) | copy-start | bytes 24580
  331.0 9.2 %copy-start.16 = (pred[256,256]{1,0:T(8,128)(4,1)S(1)}, pred[256,256]{1,0:T(8,128)(4,1)}, u32[]{:S(2)}) copy-start(pred[256,256]{1,0:T(8,128)(4,1)} %copy-done.15) | copy-start | bytes 196612
  331.0 9.2 %copy-start.24 = (f32[1,2,2,128]{3,1,2,0:T(2,128)S(1)}, f32[1,2,2,128]{3,1,2,0:T(2,128)}, u32[]{:S(2)}) copy-start(f32[1,2,2,128]{3,1,2,0:T(2,128)} %copy-done.23) | copy-start | bytes 6148
  331.0 83.0 %all-to-all-start.1 = ((bf16[32,48,2048]{2,1,0:T(8,128)(2,1)}), bf16[32,48,2048]{2,1,0:T(8,128)(2,1)}, u32[]{:S(2)}, u32[]{:S(2)}) async-start(bf16[32,48,2048]{2,1,0:T(8,128)(2,1)} %convolution_convert_fusion), calls=%async_computation.1 | async-start | bytes 12582912 | tf_op jit(solution)/shard_map/all_to_all | solution.py:155
  336.1 198.1 %reduce-scatter.2.cloned.1.call-start = ((), (), s32[]{:S(2)}) async-start(), calls=%async_computation.3 | async-start | bytes 1179648 | tf_op jit(solution)/shard_map/reduce_scatter | solution.py:169
  460.4 7.0 %copy-start.25 = (f32[256,1]{0,1:T(1,128)S(1)}, f32[256,1]{0,1:T(1,128)}, u32[]{:S(2)}) copy-start(f32[256,1]{0,1:T(1,128)} %get-tuple-element.350) | copy-start | bytes 3076
  472.1 52.9 %copy-start.9 = (bf16[256,2,128]{2,1,0:T(2,128)(2,1)S(1)}, bf16[256,2,128]{2,1,0:T(2,128)(2,1)}, u32[]{:S(2)}) copy-start(bf16[256,2,128]{2,1,0:T(2,128)(2,1)} %copy-done.8) | copy-start | bytes 393220
  472.1 53.3 %copy-start.4 = (f32[2,256,256]{2,1,0:T(8,128)S(1)}, f32[2,256,256]{2,1,0:T(8,128)}, u32[]{:S(2)}) copy-start(f32[2,256,256]{2,1,0:T(8,128)} %copy-done.3) | copy-start | bytes 1572868
  472.1 53.3 %copy-start.7 = (bf16[256,256]{0,1:T(8,128)(2,1)S(1)}, bf16[256,256]{0,1:T(8,128)(2,1)}, u32[]{:S(2)}) copy-start(bf16[256,256]{0,1:T(8,128)(2,1)} %copy-done.6) | copy-start | bytes 393220
  526.3 9.5 %copy-start.1 = (bf16[2048,3,256]{2,0,1:T(8,128)(2,1)S(1)}, bf16[2048,3,256]{2,0,1:T(8,128)(2,1)}, u32[]{:S(2)}) copy-start(bf16[2048,3,256]{2,0,1:T(8,128)(2,1)} %param.20) | copy-start | bytes 9437188
Sparse Core Ops, SparseCore 0:
  18.4 55.4 all-gather.7
  108.9 91.7 all-gather.9
  235.4 87.3 all-gather.11
  472.2 35.2 reduce-scatter.1
